TPU v7x, 256 devices: a whole 4x4x8 slice. The times are simulated.
256 devices in a mesh: frames: 32 (over y, z_lo, x), space: 8 (over z_hi, core).
Axes of the slice: x: 4, y: 4, z: 8 (z_hi: 4, z_lo: 2; z = z_hi * 2 + z_lo), core: 2. Of those that a mesh axis runs over, the one named last changes fastest.
Arguments:
- latents: bfloat16 [32, 3584, 1152], P('frames', 'space'), may hold values from -6 to 6
- merge_slot: int32 [32, 3584], P('frames', 'space'), may hold values from 0 to 1791, as said below
- modulation: float32 [6, 1152], replicated, may hold values from -3 to 3
- spatial_qkv: bfloat16 [1152, 1728], replicated, may hold values from -0.41247896 to 0.41247896
- spatial_proj: bfloat16 [576, 1152], replicated, may hold values from -0.25 to 0.25
- temporal_qkv: bfloat16 [1152, 1728], replicated, may hold values from -0.41247896 to 0.41247896
- temporal_proj: bfloat16 [576, 1152], replicated, may hold values from -0.25 to 0.25
Outputs:
- block_out: bfloat16 [32, 3584, 1152], P('frames', 'space')
Inputs may be any that keep to these rules, and one draw needn't show every extreme that they name: `merge_slot`: within each frame, the tokens of the k-th aligned block of 448 tokens join merged tokens k * 224 to (k + 1) * 224 - 1 only, and every merged token is joined by at least one token.
All inputs are finite; a program needn't handle non-finite values.
Results may differ from a plain program's by a relative error of at most 0.0062.
Values may be sent and summed in bfloat16 or wider, within the bound.
A program may use at most 128 MiB of HBM per device.

v0:
```python
import math

import jax
import jax.numpy as jnp
from jax import lax
from jax.sharding import PartitionSpec as P

HEADS = 8
HD = 72


def layer_norm(values):
    values = values.astype(jnp.float32)
    center = values - jnp.mean(values, -1, keepdims=True)
    spread = jnp.mean(center * center, -1, keepdims=True)
    return center * lax.rsqrt(spread + 1e-06)


def modulate(values, modulation, which):
    return (layer_norm(values) * (1.0 + modulation[which + 1]) + modulation[which]).astype(
        jnp.bfloat16
    )


def shards(latents, merge_slot, modulation, spatial_qkv, spatial_proj, temporal_qkv, temporal_proj):
    row_count = latents.shape[1]
    slot_count = row_count // 2
    width = latents.shape[2]
    inner = spatial_proj.shape[0]
    root_size = math.sqrt(HD)
    own_rows = latents[0]
    normed = modulate(own_rows, modulation, 0)
    local_slot = merge_slot[0] - lax.axis_index("space") * slot_count
    one_hot = (local_slot[:, None] == jnp.arange(slot_count, dtype=jnp.int32)[None, :]).astype(
        jnp.bfloat16
    )
    counts = jnp.sum(one_hot.astype(jnp.float32), 0)
    summed = lax.dot_general(
        one_hot, normed, (((0,), (0,)), ((), ())), preferred_element_type=jnp.float32
    )
    merged = (summed / counts[:, None]).astype(jnp.bfloat16)
    projected = jnp.dot(merged, spatial_qkv, preferred_element_type=jnp.float32).astype(
        jnp.bfloat16
    )
    query_rows = projected[:, :inner]
    key_rows = projected[:, inner : 2 * inner]
    value_rows = projected[:, 2 * inner :]
    query_heads = query_rows.reshape(slot_count, HEADS, HD)
    pieces = (
        lax.all_gather(key_rows, "space", axis=0, tiled=True),
        lax.all_gather(value_rows, "space", axis=0, tiled=True),
    )
    run_peak = jnp.full((HEADS, slot_count), -1e30, jnp.float32)
    key_part = pieces[0].reshape(pieces[0].shape[0], HEADS, HD)
    value_part = pieces[1].reshape(pieces[1].shape[0], HEADS, HD)
    scores = (
        jnp.einsum("qhd,khd->hqk", query_heads, key_part, preferred_element_type=jnp.float32)
        / root_size
    )
    new_peak = jnp.maximum(run_peak, jnp.max(scores, -1))
    weights = jnp.exp(scores - new_peak[..., None])
    run_total = jnp.sum(weights, -1)
    run_sum = jnp.einsum(
        "hqk,khd->hqd", weights.astype(jnp.bfloat16), value_part, preferred_element_type=jnp.float32
    )
    run_peak, run_total, run_sum = (new_peak, run_total, run_sum)
    attended = (
        (run_sum / run_total[..., None])
        .transpose(1, 0, 2)
        .reshape(slot_count, inner)
        .astype(jnp.bfloat16)
    )
    spatial_out = jnp.dot(attended, spatial_proj, preferred_element_type=jnp.float32).astype(
        jnp.bfloat16
    )
    spread_back = jnp.dot(one_hot, spatial_out, preferred_element_type=jnp.float32)
    after_spatial = (own_rows.astype(jnp.float32) + modulation[2] * spread_back).astype(
        jnp.bfloat16
    )
    by_place = lax.all_to_all(
        after_spatial[None], "frames", split_axis=1, concat_axis=0, tiled=True
    )
    frame_count = by_place.shape[0]
    place_count = by_place.shape[1]
    flat = by_place.reshape(frame_count * place_count, width)
    normed_time = modulate(flat, modulation, 3)
    projected_time = jnp.dot(normed_time, temporal_qkv, preferred_element_type=jnp.float32).astype(
        jnp.bfloat16
    )
    split = projected_time.reshape(frame_count, place_count, 3, HEADS, HD)
    scores_time = (
        jnp.einsum(
            "flhd,glhd->lhfg", split[:, :, 0], split[:, :, 1], preferred_element_type=jnp.float32
        )
        / root_size
    )
    weights_time = jnp.exp(scores_time - jnp.max(scores_time, -1, keepdims=True))
    total_time = jnp.sum(weights_time, -1)
    mixture_time = (
        jnp.einsum(
            "lhfg,glhd->flhd",
            weights_time.astype(jnp.bfloat16),
            split[:, :, 2],
            preferred_element_type=jnp.float32,
        )
        / total_time.transpose(2, 0, 1)[..., None]
    )
    attended_time = mixture_time.astype(jnp.bfloat16).reshape(frame_count * place_count, inner)
    branch = jnp.dot(attended_time, temporal_proj, preferred_element_type=jnp.float32)
    finished = (
        (flat.astype(jnp.float32) + modulation[5] * branch)
        .astype(jnp.bfloat16)
        .reshape(frame_count, place_count, width)
    )
    return lax.all_to_all(finished, "frames", split_axis=0, concat_axis=1, tiled=True)


def solution(mesh):
    placed = (P("frames", "space", None), P("frames", "space"), P(), P(), P(), P(), P())
    return jax.shard_map(
        shards, mesh=mesh, in_specs=placed, out_specs=P("frames", "space", None), check_vma=False
    )
```

profile of v0, /device:TPU:1, one launch (start us, length us, event | category | flops | bytes accessed | tf_op | source)
XLA Modules:
  0.0 201.3 jit_solution(2372403140848422935)
XLA Ops:
  6.5 1.8 slice_reduce_fusion.1
  10.6 1.6 fusion.16
  12.3 4.1 %convolution_convert_fusion.2 = bf16[224,1728]{1,0:T(8,128)(2,1)S(1)} fusion(bf16[1152,1728]{0,1:T(8,128)(2,1)} %param.10, bf16[1,448,1152]{2,1,0:T(8,128)(2,1)S(1)} %copy-done.2, f32[1152]{0:T(1024)S(1)} %get-tuple-element.6, f32[1152]{0:T(1024)S(1)} %get-tuple-element.7, f32[448]{0:T(512)S(1)} %add_rsqrt_fusion.1, f32[448]{0:T(512)S(1)} %broadcast_multiply_fusion.1, ...), kind=kOutput, calls=%fused_computation.24 | convolution fusion | flops 1127124992 | bytes 5803136 | tf_op jit(solution)/shard_map/dot_general | solution.py:42
  18.9 40.6 %all-gather.3.cloned.1.call-done = bf16[1792,576]{1,0:T(8,128)(2,1)} async-done(((bf16[224,576]{1,0:T(8,128)(2,1)}), bf16[1792,576]{1,0:T(8,128)(2,1)}) %all-gather.3.cloned.1.call-update) | async-done | bytes 2064400 | tf_op jit(solution)/shard_map/all_gather | solution.py:50
  59.6 3.0 %copy.34 = bf16[1792,576]{0,1:T(8,128)(2,1)S(1)} copy(bf16[1792,576]{1,0:T(8,128)(2,1)} %all-gather.3.cloned.1.call-done) | data formatting | bytes 4128768 | tf_op jit(solution)/shard_map/all_gather | solution.py:50
  62.6 2.9 %multiply_reduce_fusion = (f32[8,224]{1,0:T(8,128)S(1)}, f32[8,224,1792]{2,1,0:T(8,128)S(1)}) fusion(bf16[224,8,72]{0,2,1:T(8,128)(2,1)} %bitcast.87, bf16[1792,8,72]{0,2,1:T(8,128)(2,1)S(1)} %bitcast.83), kind=kOutput, calls=%fused_computation.1 | convolution fusion | flops 468842752 | bytes 15174656 | tf_op jit(solution)/shard_map/qhd,khd->hqk/dot_general | solution.py:57
  65.5 4.6 %copy-done.1 = f32[8,224,1792]{2,1,0:T(8,128)} copy-done((f32[8,224,1792]{2,1,0:T(8,128)}, f32[8,224,1792]{2,1,0:T(8,128)S(1)}, u32[]{:S(2)}) %copy-start.1) | copy-done | bytes 12845080
  70.1 2.3 %fusion = f32[8,224]{1,0:T(8,128)S(1)} fusion(f32[8,224,1792]{2,1,0:T(8,128)S(1)} %get-tuple-element.20, f32[8,224]{1,0:T(8,128)S(1)} %broadcast_maximum_fusion), kind=kLoop, calls=%fused_computation.2 | loop fusion | flops 9632000 | bytes 12859392 | tf_op jit(solution)/shard_map/reduce_sum | solution.py:62
  72.4 24.5 %all-gather.5.cloned.1.call-done = bf16[1792,576]{1,0:T(8,128)(2,1)} async-done(((bf16[224,576]{1,0:T(8,128)(2,1)}), bf16[1792,576]{1,0:T(8,128)(2,1)}) %all-gather.5.cloned.1.call-update) | async-done | bytes 2064400 | tf_op jit(solution)/shard_map/all_gather | solution.py:51
  96.9 4.1 %copy.35 = bf16[1792,576]{0,1:T(8,128)(2,1)} copy(bf16[1792,576]{1,0:T(8,128)(2,1)} %all-gather.5.cloned.1.call-done) | data formatting | bytes 4128768 | tf_op jit(solution)/shard_map/all_gather | solution.py:51
  101.0 7.8 %fusion.45 = bf16[224,8,72]{0,2,1:T(8,128)(2,1)S(1)} fusion(bf16[1792,8,72]{0,2,1:T(8,128)(2,1)} %bitcast.86, f32[8,224,1792]{2,1,0:T(8,128)} %copy-done.1, f32[8,224]{1,0:T(8,128)S(1)} %broadcast_maximum_fusion, f32[224,8]{0,1:T(8,128)S(1)} %bitcast.89), kind=kOutput, calls=%fused_computation.54 | convolution fusion | flops 472313856 | bytes 15181824 | tf_op jit(solution)/shard_map/hqk,khd->hqd/dot_general | solution.py:63
  108.9 2.0 fusion.10
  110.8 2.8 %copy.59 = bf16[1,448,1152]{2,0,1:T(2,128)(2,1)S(1)} copy(bf16[1,448,1152]{2,1,0:T(8,128)(2,1)} %fusion.10) | data formatting | bytes 2064384 | tf_op jit(solution)/shard_map/broadcast_in_dim | solution.py:81
  114.2 7.9 %reduce.17 = bf16[448,1152]{1,0:T(8,128)(2,1)} reduce(bf16[448,1,1152]{2,1,0:T(2,128)(2,1)S(1)} %bitcast.84, bf16[]{:T(256)} %broadcast.86), dimensions={1}, to_apply=%bitcast.82.reduce_sub_computation | reduce | bytes 2064386
  122.2 2.5 %reshape.108 = bf16[32,2,8064]{2,1,0:T(2,128)(2,1)S(1)} reshape(bf16[448,1152]{1,0:T(8,128)(2,1)} %reduce.17) | data formatting | bytes 2064384
  124.6 22.3 %all_to_all.21 = bf16[32,2,8064]{2,1,0:T(2,128)(2,1)} all-to-all(bf16[32,2,8064]{2,1,0:T(2,128)(2,1)S(1)} %reshape.108), channel_id=1, replica_groups=mesh['frames'=32,'space'=8] {'frames'}, dimensions={0} | all-to-all | bytes 2064384 | tf_op jit(solution)/shard_map/all_to_all | solution.py:80
  146.9 4.2 %reshape.109 = bf16[448,1,1152]{2,1,0:T(2,128)(2,1)S(1)} reshape(bf16[32,2,8064]{2,1,0:T(2,128)(2,1)} %all_to_all.21) | data formatting | bytes 2064384
  153.6 2.5 %convolution_convert_fusion = bf16[448,1728]{1,0:T(8,128)(2,1)S(1)} fusion(bf16[1152,1728]{0,1:T(8,128)(2,1)S(1)} %copy-done.9, bf16[1,448,1152]{2,1,0:T(8,128)(2,1)S(1)} %get-tuple-element.12, f32[1152]{0:T(1024)S(1)} %copy-done.6, f32[1152]{0:T(1024)S(1)} %copy-done.7, f32[448]{0:T(512)S(1)} %add_rsqrt_fusion, f32[448]{0:T(512)S(1)} %broadcast_multiply_fusion), kind=kOutput, calls=%fused_computation.14 | convolution fusion | flops 1787498496 | bytes 6574592 | tf_op jit(solution)/shard_map/dot_general | solution.py:87
  156.1 4.0 %reshape.98 = bf16[32,14,3,8,72]{4,3,2,1,0:T(8,128)(2,1)} reshape(bf16[448,1728]{1,0:T(8,128)(2,1)S(1)} %convolution_convert_fusion) | data formatting | bytes 3096576 | tf_op jit(solution)/shard_map/reshape | solution.py:90
  160.1 1.9 fusion.61
  164.7 1.5 reshape.99
  166.2 2.5 %fusion.8 = bf16[448,1152]{1,0:T(8,128)(2,1)S(1)} fusion(bf16[448,576]{1,0:T(8,128)(2,1)} %reshape.99, bf16[576,1152]{1,0:T(8,128)(2,1)} %param.13, bf16[1,448,1152]{2,1,0:T(8,128)(2,1)S(1)} %copy-done.5, f32[1152]{0:T(1024)S(1)} %get-tuple-element.5), kind=kOutput, calls=%fused_computation.15 | convolution fusion | flops 596606976 | bytes 3912192 | tf_op jit(solution)/shard_map/dot_general | solution.py:109
  169.1 23.2 %all_to_all.22 = bf16[32,14,1152]{2,1,0:T(8,128)(2,1)} all-to-all(bf16[32,14,1152]{2,1,0:T(8,128)(2,1)S(1)} %reshape.100), channel_id=1, replica_groups=mesh['frames'=32,'space'=8] {'frames'}, dimensions={0} | all-to-all | bytes 2064384 | tf_op jit(solution)/shard_map/all_to_all | solution.py:115
  192.3 2.2 %all_to_all.8 = bf16[1,448,1152]{2,1,0:T(8,128)(2,1)} reshape(bf16[32,14,1152]{2,1,0:T(8,128)(2,1)} %all_to_all.22) | data formatting | bytes 2064384 | tf_op jit(solution)/shard_map/all_to_all | solution.py:115
  (41 shorter events, 11.0 us)
Async XLA Ops:
  6.5 102.3 %copy-start = (bf16[576,1152]{1,0:T(8,128)(2,1)S(1)}, bf16[576,1152]{1,0:T(8,128)(2,1)}, u32[]{:S(2)}) copy-start(bf16[576,1152]{1,0:T(8,128)(2,1)} %param.11) | copy-start | bytes 3981316
  6.5 5.7 %copy-start.2 = (bf16[1,448,1152]{2,1,0:T(8,128)(2,1)S(1)}, bf16[1,448,1152]{2,1,0:T(8,128)(2,1)}, u32[]{:S(2)}) copy-start(bf16[1,448,1152]{2,1,0:T(8,128)(2,1)} %param.7) | copy-start | bytes 3096580
  6.5 53.0 %all-gather.3.cloned.1.call-start = ((), (), s32[]{:S(2)}) async-start(), calls=%async_computation.2 | async-start | bytes 2580480 | tf_op jit(solution)/shard_map/all_gather | solution.py:50
  17.3 79.6 %all-gather.5.cloned.1.call-start = ((), (), s32[]{:S(2)}) async-start(), calls=%async_computation.3 | async-start | bytes 2580480 | tf_op jit(solution)/shard_map/all_gather | solution.py:51
  65.5 4.6 %copy-start.1 = (f32[8,224,1792]{2,1,0:T(8,128)}, f32[8,224,1792]{2,1,0:T(8,128)S(1)}, u32[]{:S(2)}) copy-start(f32[8,224,1792]{2,1,0:T(8,128)S(1)} %get-tuple-element.20) | copy-start | bytes 38535172
  101.0 7.8 %copy-start.3 = (bf16[1,448,1152]{2,1,0:T(8,128)(2,1)S(1)}, bf16[1,448,1152]{2,1,0:T(8,128)(2,1)}, u32[]{:S(2)}) copy-start(bf16[1,448,1152]{2,1,0:T(8,128)(2,1)} %param.7) | copy-start | bytes 3096580
  101.0 7.8 %copy-start.8 = (f32[1152]{0:T(1024)S(1)}, f32[1152]{0:T(1024)}, u32[]{:S(2)}) copy-start(f32[1152]{0:T(1024)} %get-tuple-element.8) | copy-start | bytes 13828
  151.1 1.2 copy-start.6
  151.1 1.2 copy-start.7
  151.1 2.5 %copy-start.9 = (bf16[1152,1728]{0,1:T(8,128)(2,1)S(1)}, bf16[1152,1728]{0,1:T(8,128)(2,1)}, u32[]{:S(2)}) copy-start(bf16[1152,1728]{0,1:T(8,128)(2,1)} %param.12) | copy-start | bytes 11943940
  151.4 1.0 copy-start.4
  164.3 1.9 copy-start.5
Sparse Core Ops, SparseCore 0:
  17.4 42.0 all-gather.2
  61.4 35.4 all-gather.4
where the time goes:
time: 202 us; the launch traced here: 201 us
  waiting for transfers between devices  65.8 us (33%)
  blocking collectives  45.5 us (23%)
  local copies, waits for them, and re-layouts  35.6 us (18%)
  matrix products  23.5 us (12%)
  other arithmetic  17.2 us (9%)
  between operations  13.6 us (7%)
    all_gather x1, waiting for transfers between devices, shards(): lax.all_gather(key_rows, 'space', axis=0, tiled=True)  40.6 us
    all_gather x1, waiting for transfers between devices, shards(): lax.all_gather(value_rows, 'space', axis=0, tiled=True)  24.5 us
    all_to_all x1, blocking collectives, shards(): lax.all_to_all(finished, 'frames', split_axis=0, concat_axis=1, tiled=True)  23.2 us
    all_to_all x1, blocking collectives, shards(): lax.all_to_all(after_spatial[None], 'frames', split_axis=1, concat_axis=0...  22.3 us
    unnamed x23, local copies, waits for them, and re-layouts  13.7 us
    unnamed x1, other arithmetic  7.93 us
    dot_general x1, matrix products, shards(): jnp.einsum('hqk,khd->hqd', weights.astype(jnp.bfloat16), value_part, pref...  7.79 us
    all_gather x1, local copies, waits for them, and re-layouts, shards(): lax.all_gather(value_rows, 'space', axis=0, tiled=True)  4.13 us
  transfers between devices with their start and end apart: 2, of which 2 were waited for; matrix products, arithmetic and copies ran while one was open for 5% of the time, Pallas kernels for 0%

commit v1 on v0

v1 whole, which is shorter than its diff:
```python
import math

import jax
import jax.numpy as jnp
from jax import lax
from jax.experimental import pallas as pl
from jax.experimental.pallas import tpu as pltpu
from jax.sharding import PartitionSpec as P

MESH = pl.DeviceIdType.MESH
D, HEADS, HD, ROWS, INNER, FRAMES, MROWS = 1152, 8, 72, 448, 576, 32, 224
ALLM = MROWS * HEADS
LOCS = 16
OWNED = FRAMES * LOCS
WIDE = 640
PACK = 256
OROW = 80
LOG2E_SCALE = math.log2(math.e) / math.sqrt(HD)
BF, F32, I32 = jnp.bfloat16, jnp.float32, jnp.int32


def iota(shape, dim):
    return lax.broadcasted_iota(I32, shape, dim)


def onehot(cond):
    return jnp.where(cond, 1.0, 0.0).astype(BF)


def dot(a, b):
    return jnp.dot(a, b, preferred_element_type=F32)


def dot_t(a, b):
    return lax.dot_general(a, b, (((1,), (1,)), ((), ())), preferred_element_type=F32)


def norm_rows(values, scale, shift):
    values = values.astype(F32)
    center = values - jnp.mean(values, -1, keepdims=True)
    spread = jnp.mean(center * center, -1, keepdims=True)
    return (center * lax.rsqrt(spread + 1e-06) * (1.0 + scale) + shift).astype(BF)


def kernel(
    slot_ref, mod_ref, lat_hbm, wsp_hbm, psp_hbm, wt_hbm, pt_hbm, out_hbm,
    lat, wsp, psp, wt, pt, normed, lat_got, lat_perm, qkv_send, qkv_got, keys, att_send, att_got,
    exp_send, exp_got, after, att_perm, ret_send, ret_got, outv, perm, unperm,
    ld_sem, lat_ss, lat_rs, qkv_ss, qkv_rs, att_ss, att_rs, exp_ss, exp_rs, ret_ss, ret_rs, out_sem,
):
    mf = lax.axis_index("frames")
    ms = lax.axis_index("space")
    my, mp = mf // 8, mf % 8
    mz, mx = mp // 4, mp % 4
    mzh, mcore = ms // 2, ms % 2

    def skipped(y):
        return ((y + mcore) % 2) * 4 + (y + 2 * mcore) % 4

    def owns(y, p):
        return p != skipped(y)

    def place(y, p):
        return y * 7 + p - jnp.where(p > skipped(y), 1, 0)

    me_owns = owns(my, mp)
    my_place = place(my, mp)

    def frame_peer(k):
        y = (my + k // 8) % 4
        p = ((mz + (k // 4) % 2) % 2) * 4 + (mx + k % 4) % 4
        return y, p

    def space_peer(k):
        kk = k // 2
        dz = jnp.where(kk == 2, 3, jnp.where(kk == 3, 0, 2 - kk))
        return 2 * ((mzh + dz) % 4) + (mcore + k % 2 + 1) % 2

    def local(src, dst, sem):
        return pltpu.make_async_copy(src, dst, sem)

    def remote(src, dst, ss, rs, f, s):
        return pltpu.make_async_remote_copy(
            src_ref=src, dst_ref=dst, send_sem=ss, recv_sem=rs, device_id=(f, s), device_id_type=MESH
        )

    def rows(ref, start, size, mult):
        return ref.at[pl.ds(pl.multiple_of(start, mult), size)]

    loads = [
        local(src, dst, ld_sem.at[n])
        for n, (src, dst) in enumerate(((lat_hbm, lat), (wsp_hbm, wsp), (psp_hbm, psp), (wt_hbm, wt), (pt_hbm, pt)))
    ]
    loads[0].start()
    barrier = pltpu.get_barrier_semaphore()

    def greet_frame(k, c):
        y, p = frame_peer(k)
        pl.semaphore_signal(barrier, inc=1, device_id=(y * 8 + p, ms), device_id_type=MESH)
        return c

    def greet_space(k, c):
        pl.semaphore_signal(barrier, inc=1, device_id=(mf, (ms + k) % 8), device_id_type=MESH)
        return c

    lax.fori_loop(1, FRAMES, greet_frame, 0)
    lax.fori_loop(1, HEADS, greet_space, 0)
    for copy in loads[1:]:
        copy.start()

    loads[0].wait()

    def norm_chunk(n, c):
        at = pl.ds(pl.multiple_of(n * 64, 64), 64)
        normed[at, :] = norm_rows(lat[at, :], mod_ref[1:2, :], mod_ref[0:1, :])
        return c

    lax.fori_loop(0, ROWS // 64, norm_chunk, 0)
    pl.semaphore_wait(barrier, FRAMES - 1 + HEADS - 1)

    def to_owners(src, got, ss, rs):
        def send(k, c):
            y, p = frame_peer(k)

            @pl.when(owns(y, p))
            def _():
                remote(
                    rows(src, place(y, p) * LOCS, LOCS, LOCS), rows(got, mf * LOCS, LOCS, LOCS),
                    ss, rs, y * 8 + p, ms,
                ).start()

            return c

        @pl.when(me_owns)
        def _():
            local(rows(src, my_place * LOCS, LOCS, LOCS), rows(got, mf * LOCS, LOCS, LOCS), rs).start()

        lax.fori_loop(1, FRAMES, send, 0)

    def drain_to_owners(src, ss):
        @pl.when(me_owns)
        def _():
            part = src.at[pl.ds(0, ROWS - LOCS)]
            local(part, part, ss).wait()

        @pl.when(jnp.logical_not(me_owns))
        def _():
            local(src, src, ss).wait()

    to_owners(lat, lat_got, lat_ss, lat_rs)

    slots = slot_ref[...] - ms * MROWS
    joins = iota((MROWS, ROWS), 0) == slots
    join_t = onehot(joins)
    counts = jnp.sum(jnp.where(joins, 1.0, 0.0), -1, keepdims=True)
    merged = (dot(join_t, normed[...]) / counts).astype(BF)
    loads[1].wait()
    proj = dot(merged, wsp[...]).astype(BF)
    tail = jnp.where(iota((MROWS, PACK - 3 * HD), 1) == 0, 1.0, 0.0).astype(BF)
    for h in range(HEADS):
        qkv_send[h * MROWS : (h + 1) * MROWS, :] = jnp.concatenate(
            [proj[:, n * INNER + h * HD : n * INNER + (h + 1) * HD] for n in range(3)] + [tail], 1
        )

    def send_qkv(k, c):
        s = space_peer(k)

        @pl.when(s != ms)
        def _():
            remote(
                rows(qkv_send, s * MROWS, MROWS, MROWS), rows(qkv_got, ms * MROWS, MROWS, MROWS),
                qkv_ss.at[s], qkv_rs.at[ms], mf, s,
            ).start()

        return c

    lax.fori_loop(0, HEADS, send_qkv, 0)
    local(rows(qkv_send, ms * MROWS, MROWS, MROWS), rows(qkv_got, ms * MROWS, MROWS, MROWS), qkv_rs.at[ms]).start()

    r, c = iota((OWNED, OWNED), 0), iota((OWNED, OWNED), 1)
    perm[...] = onehot((r // FRAMES == c % LOCS) & (r % FRAMES == c // LOCS))
    unperm[...] = onehot((c // FRAMES == r % LOCS) & (c % FRAMES == r // LOCS))
    join = dot_t(onehot(iota((ROWS, ROWS), 0) == iota((ROWS, ROWS), 1)), join_t).astype(BF)
    shift = onehot((iota((PACK, PACK), 0) == iota((PACK, PACK), 1) + HD) & (iota((PACK, PACK), 1) < HD))
    pick = onehot((iota((OROW, PACK), 0) + 2 * HD == iota((OROW, PACK), 1)) & (iota((OROW, PACK), 0) < HD))
    cr, cc = iota((INNER, HEADS * OROW), 0), iota((INNER, HEADS * OROW), 1)
    compact = onehot((cr // HD) * OROW + cr % HD == cc)
    exp_send[:, INNER:] = jnp.zeros((ROWS, WIDE - INNER), BF)
    att_send[...] = jnp.zeros((HEADS * OROW, PACK), BF)

    @pl.when(me_owns)
    def _():
        local(lat_got, lat_got, lat_rs).wait()
        lat_perm[...] = dot(perm[...], lat_got[...]).astype(BF)

    def take_qkv(k, c):
        part = rows(qkv_got, k * MROWS, MROWS, MROWS)
        local(part, part, qkv_rs.at[k]).wait()
        at = pl.ds(pl.multiple_of(k * MROWS, MROWS), MROWS)
        keys[at, :] = dot(qkv_got[at, :], shift).astype(BF)
        return c

    lax.fori_loop(0, HEADS, take_qkv, 0)

    def attend(k, c):
        s = space_peer(k)
        q = qkv_got[pl.ds(pl.multiple_of(s * MROWS, MROWS), MROWS), :]
        scores = dot_t(q, keys[...])
        peak = jnp.max(scores, -1, keepdims=True)
        weights = jnp.exp2((scores - peak) * LOG2E_SCALE).astype(BF)
        mixed = dot(weights, qkv_got[...])
        mixed = (mixed / mixed[:, 3 * HD : 3 * HD + 1]).astype(BF)
        att_send[pl.ds(pl.multiple_of(s * OROW, OROW), OROW), 0:MROWS] = dot_t(pick, mixed).astype(BF)

        @pl.when(s != ms)
        def _():
            remote(
                rows(att_send, s * OROW, OROW, OROW), rows(att_got, ms * OROW, OROW, OROW),
                att_ss.at[s], att_rs.at[ms], mf, s,
            ).start()

        @pl.when(s == ms)
        def _():
            local(rows(att_send, ms * OROW, OROW, OROW), rows(att_got, ms * OROW, OROW, OROW), att_rs.at[ms]).start()

        return c

    lax.fori_loop(0, HEADS, attend, 0)

    def take_att(k, c):
        part = rows(att_got, k * OROW, OROW, OROW)
        local(part, part, att_rs.at[k]).wait()
        return c

    lax.fori_loop(0, HEADS, take_att, 0)
    attended = dot(compact, att_got[:, 0:MROWS]).astype(BF)
    exp_send[:, 0:INNER] = dot_t(join, attended).astype(BF)
    to_owners(exp_send, exp_got, exp_ss, exp_rs)
    loads[2].wait()

    def own_after(n, c):
        at = pl.ds(pl.multiple_of(n * MROWS, MROWS), MROWS)
        branch = dot(exp_send[at, 0:INNER], psp[...]).astype(BF).astype(F32)
        after[at, :] = (lat[at, :].astype(F32) + mod_ref[2:3, :] * branch).astype(BF)
        return c

    lax.fori_loop(0, 2, own_after, 0)
    loads[3].wait()
    loads[4].wait()

    @pl.when(me_owns)
    def _():
        local(exp_got, exp_got, exp_rs).wait()
        near = iota((128, 128), 0) // FRAMES == iota((128, 128), 1) // FRAMES

        def chunk(n, c):
            at = pl.ds(pl.multiple_of(n * 256, 256), 256)
            mine = dot(perm[at, :], exp_got[:, 0:INNER]).astype(BF)
            branch = dot(mine, psp[...]).astype(BF).astype(F32)
            tokens = (lat_perm[at, :].astype(F32) + mod_ref[2:3, :] * branch).astype(BF)
            tokens = norm_rows(tokens, mod_ref[4:5, :], mod_ref[3:4, :])
            inner = dot(tokens, wt[...]).astype(BF)
            for b in range(2):
                part = inner[b * 128 : (b + 1) * 128]
                q, k, v = (part[:, i * INNER : (i + 1) * INNER] for i in range(3))
                tiles = [None] * 5
                for pair in range(4):
                    base = pair * 128
                    width = min(256, INNER - base)
                    lane = iota((128, width), 1) + base
                    total = jnp.zeros((128, width), F32)
                    for h in (2 * pair, 2 * pair + 1):
                        own = (lane >= h * HD) & (lane < (h + 1) * HD)
                        qh = jnp.where(own, q[:, base : base + width].astype(F32), 0.0).astype(BF)
                        scores = jnp.where(near, dot_t(qh, k[:, base : base + width]), -1e30)
                        peak = jnp.max(scores, -1, keepdims=True)
                        weights = jnp.exp2((scores - peak) * LOG2E_SCALE)
                        row_total = jnp.sum(weights, -1, keepdims=True)
                        mixed = dot(weights.astype(BF), v[:, base : base + width])
                        total = jnp.where(own, mixed / row_total, total)
                    for t, piece in ((pair, total[:, :128]), (pair + 1, total[:, 128:])):
                        tiles[t] = piece if tiles[t] is None else tiles[t] + piece
                dst = pl.ds(pl.multiple_of(n * 256 + b * 128, 128), 128)
                for t in range(4):
                    att_perm[dst, t * 128 : (t + 1) * 128] = tiles[t].astype(BF)
                att_perm[dst, 512:INNER] = tiles[4].astype(BF)
            return c

        lax.fori_loop(0, 2, chunk, 0)

        def unpermute(n, c):
            at = pl.ds(pl.multiple_of(n * 256, 256), 256)
            ret_send[at, 0:INNER] = dot(unperm[at, :], att_perm[:, 0:INNER]).astype(BF)
            ret_send[at, INNER:] = jnp.zeros((256, WIDE - INNER), BF)
            return c

        lax.fori_loop(0, 2, unpermute, 0)

        def send_back(k, c):
            y, p = frame_peer(k)
            f = y * 8 + p
            remote(
                rows(ret_send, f * LOCS, LOCS, LOCS), rows(ret_got, my_place * LOCS, LOCS, LOCS),
                ret_ss, ret_rs, f, ms,
            ).start()
            return c

        local(rows(ret_send, mf * LOCS, LOCS, LOCS), rows(ret_got, my_place * LOCS, LOCS, LOCS), ret_rs).start()
        lax.fori_loop(1, FRAMES, send_back, 0)

    local(ret_got, ret_got, ret_rs).wait()

    def finish(n, c):
        at = pl.ds(pl.multiple_of(n * MROWS, MROWS), MROWS)
        branch = dot(ret_got[at, 0:INNER], pt[...])
        outv[at, :] = (after[at, :].astype(F32) + mod_ref[5:6, :] * branch).astype(BF)
        local(outv.at[at], out_hbm.at[at], out_sem.at[n]).start()
        return c

    lax.fori_loop(0, 2, finish, 0)

    drain_to_owners(lat, lat_ss)
    drain_to_owners(exp_send, exp_ss)

    @pl.when(me_owns)
    def _():
        part = ret_send.at[pl.ds(0, OWNED - LOCS)]
        local(part, part, ret_ss).wait()

    def drain_space(k, c):
        s = (ms + k) % 8
        part = rows(qkv_send, s * MROWS, MROWS, MROWS)
        local(part, part, qkv_ss.at[s]).wait()
        part = rows(att_send, s * OROW, OROW, OROW)
        local(part, part, att_ss.at[s]).wait()
        return c

    lax.fori_loop(1, HEADS, drain_space, 0)

    def drain_out(n, c):
        at = pl.ds(pl.multiple_of(n * MROWS, MROWS), MROWS)
        local(outv.at[at], out_hbm.at[at], out_sem.at[n]).wait()
        return c

    lax.fori_loop(0, 2, drain_out, 0)


def shards(latents, merge_slot, modulation, spatial_qkv, spatial_proj, temporal_qkv, temporal_proj):
    vmem = pl.BlockSpec(memory_space=pltpu.VMEM)
    hbm = pl.BlockSpec(memory_space=pl.ANY)
    dma = pltpu.SemaphoreType.DMA
    sizes = (
        (ROWS, D), (D, 3 * INNER), (INNER, D), (D, 3 * INNER), (INNER, D), (ROWS, D), (OWNED, D), (OWNED, D),
        (ALLM, PACK), (ALLM, PACK), (ALLM, PACK), (HEADS * OROW, PACK), (HEADS * OROW, PACK),
        (ROWS, WIDE), (OWNED, WIDE), (ROWS, D), (OWNED, WIDE), (OWNED, WIDE), (ROWS, WIDE), (ROWS, D),
        (OWNED, OWNED), (OWNED, OWNED),
    )
    one = dma(())
    many = dma((HEADS,))
    out = pl.pallas_call(
        kernel,
        out_shape=jax.ShapeDtypeStruct((ROWS, D), BF),
        in_specs=[vmem, vmem] + [hbm] * 5,
        out_specs=hbm,
        scratch_shapes=[pltpu.VMEM(size, BF) for size in sizes]
        + [dma((5,)), one, one, many, many, many, many, one, one, one, one, dma((2,))],
        compiler_params=pltpu.CompilerParams(
            collective_id=0, has_side_effects=True, vmem_limit_bytes=62 * 1024 * 1024
        ),
    )(merge_slot, modulation, latents[0], spatial_qkv, spatial_proj, temporal_qkv, temporal_proj)
    return out[None]


def solution(mesh):
    placed = (P("frames", "space", None), P("frames", "space"), P(), P(), P(), P(), P())
    return jax.shard_map(
        shards, mesh=mesh, in_specs=placed, out_specs=P("frames", "space", None), check_vma=False
    )
```

time: 202 us -> 104 us (0.51)
  Pallas kernels: 0 us -> 88.3 us
  waiting for transfers between devices: 65.8 us -> 0 us
  blocking collectives: 45.5 us -> 0 us
  matrix products: 23.5 us -> 0 us
  local copies, waits for them, and re-layouts: 35.6 us -> 15.2 us
  other arithmetic: 17.2 us -> 0 us
  between operations: 13.6 us -> 0.01 us
    pallas_call x0 -> x1, Pallas kernels: none -> 88.3 us  [shards(): pl.pallas_call(kernel, out_shape=jax.ShapeDtypeStruct((ROWS, D), BF), in_...]
    all_gather x2 -> x0, waiting for transfers between devices: 65.1 us -> none  [the longest x1 40.6 us: shards(): lax.all_gather(key_rows, 'space', axis=0, tiled=True)]
    all_to_all x2 -> x0, blocking collectives: 45.5 us -> none  [the longest x1 23.2 us: shards(): lax.all_to_all(finished, 'frames', split_axis=0, concat_axis=1, tiled=True)]
    dot_general x8 -> x0, matrix products: 23.5 us -> none  [the longest x1 7.79 us: shards(): jnp.einsum('hqk,khd->hqd', weights.astype(jnp.bfloat16), value_part, pref...]
    unnamed x1 -> x0, other arithmetic: 7.93 us -> none
    all_gather x2 -> x0, local copies, waits for them, and re-layouts: 7.11 us -> none  [the longest x1 4.13 us: shards(): lax.all_gather(value_rows, 'space', axis=0, tiled=True)]
    reduce_sum x7 -> x0, other arithmetic: 6.73 us -> none  [the longest x1 2.28 us: shards(): run_total = jnp.sum(weights, -1)]
    reshape x3 -> x0, local copies, waits for them, and re-layouts: 5.83 us -> none  [the longest x1 3.98 us: shards(): split = projected_time.reshape(frame_count, place_count, 3, HEADS, HD)]
  transfers between devices with their start and end apart: 2 -> 0, of which waited for: 2 -> 0; matrix products, arithmetic and copies ran while one was open for 5% -> 0% of each run, Pallas kernels for 0% -> 0%
where the time goes in v1:
time: 104 us; the launch traced here: 103 us
  Pallas kernels  88.3 us (85%)
  local copies, waits for them, and re-layouts  15.2 us (15%)
    pallas_call x1, Pallas kernels, shards(): pl.pallas_call(kernel, out_shape=jax.ShapeDtypeStruct((ROWS, D), BF), in_...  88.3 us
    unnamed x3, local copies, waits for them, and re-layouts  15.2 us

profile of v1, /device:TPU:1, one launch (start us, length us, event | category | flops | bytes accessed | tf_op | source)
XLA Modules:
  0.0 103.5 jit_solution(14896861384375432329)
XLA Ops:
  0.0 6.4 %copy.8.wsp_hbm = bf16[1152,1728]{1,0:T(8,128)(2,1)} copy(bf16[1152,1728]{0,1:T(8,128)(2,1)} %param.10) | data formatting | bytes 7962624 | tf_op args[3]
  6.4 6.5 %copy.9.wt_hbm = bf16[1152,1728]{1,0:T(8,128)(2,1)} copy(bf16[1152,1728]{0,1:T(8,128)(2,1)} %param.12) | data formatting | bytes 7962624 | tf_op args[5]
  12.9 88.3 %shard_map.73 = bf16[448,1152]{1,0:T(8,128)(2,1)} custom-call(s32[1,448]{1,0:T(1,128)} %slot_ref.1, f32[6,1152]{1,0:T(8,128)} %mod_ref.1, bf16[448,1152]{1,0:T(8,128)(2,1)} %bitcast.3, bf16[1152,1728]{1,0:T(8,128)(2,1)} %copy.8.wsp_hbm, bf16[576,1152]{1,0:T(8,128)(2,1)} %psp_hbm.1, bf16[1152,1728]{1,0:T(8,128)(2,1)} %copy.9.wt_hbm, bf16[576,1152]{1,0:T(8,128)(2,1)} %pt_hbm.1), custom_call_target="tpu_custom_call" | custom-call | tf_op jit(solution)/shard_map/pallas_call | solution.py:360
  101.2 2.3 %copy.11 = bf16[1,448,1152]{2,1,0:T(8,128)(2,1)} copy(bf16[1,448,1152]{2,1,0:T(8,128)(2,1)} %bitcast.2) | data formatting | bytes 2064384
